TPU v7x, 32 devices: a whole 2x2x4 slice. The times are simulated.
32 devices in a mesh: box: 2 (over y), gx: 8 (over z, x), gy: 2 (over core).
Axes of the slice: x: 2, y: 2, z: 4, core: 2. Of those that a mesh axis runs over, the one named last changes fastest.
Arguments:
- positions: float32 [16, 4, 3, 256], P(('box', 'gx'), 'gy'), parts along dimension 0, may hold values from 0 to 18, as said below
- polarizability: float32 [16, 4, 256], P(('box', 'gx'), 'gy'), parts along dimension 0, may hold values from 0.3 to 1.5
- tile_counts: int32 [16, 4, 2], P(('box', 'gx'), 'gy'), parts along dimension 0, may hold values from 80 to 128, as said below
- molecules: int32 [16, 4, 256], P(('box', 'gx'), 'gy'), parts along dimension 0, may hold values from 0 to 170, as said below
- perm_field: float32 [16, 4, 3, 256], P(('box', 'gx'), 'gy'), parts along dimension 0, may hold values from -6 to 6
- dipoles: float32 [16, 4, 3, 256], P(('box', 'gx'), 'gy'), parts along dimension 0, may hold values from -4 to 4
- past_out: float32 [16, 4, 7, 3, 256], P(('box', 'gx'), 'gy'), parts along dimension 0, may hold values from -4 to 4
- past_res: float32 [16, 4, 7, 3, 256], P(('box', 'gx'), 'gy'), parts along dimension 0, may hold values from -15 to 15
Outputs:
- dipoles_next: float32 [16, 4, 3, 256], P(('box', 'gx'), 'gy'), parts along dimension 0
- diis_weights: float32 [16], P('box'), parts along dimension 0
There are 2 independent parts, one for each index of `box`. A program takes and returns all parts, laid end to end along the dimension named above; each array names one. Nothing has to cross between parts.
Inputs may be any that keep to these rules, and one draw needn't show every extreme that they name: x and y in [0, 9); z of an atom in z-tile t lies in [9 t, 9 t + 9); padded slots carry positions too. `tile_counts`: some z-tile is full. `molecules`: a group holds at most three atoms, all of one z-tile of one cell.
All inputs are finite; a program needn't handle non-finite values.
Results may differ from a plain program's by a relative error of at most 0.0003.
Values sent between devices are 32-bit elements; how exact they have to be, the bound alone decides.
A program may use at most 64 MiB of HBM per device.

v0:
```python
import jax
import jax.numpy as jnp
from jax import lax
from jax.sharding import PartitionSpec as P

ITERS = 2
CELL_SIDE = 9.0
CUTOFF_SQ = 81.0
SOFTENING = 0.25
THOLE_DAMP = 0.39
FAR_LIFT = 1000.0
NEIGHBOUR_X = (1.0, 0.0, 1.0, 1.0)
NEIGHBOUR_Y = (0.0, 1.0, 1.0, -1.0)


def from_behind(block, axis, distance):
    devices = range(lax.axis_size(axis))
    route = [((i - distance) % len(devices), i) for i in devices]
    return lax.ppermute(block, axis, route)


def pair_terms(
    target_coords,
    target_polar,
    target_groups,
    target_occupied,
    source_coords,
    source_polar,
    source_groups,
    source_occupied,
):
    displace = source_coords[:, None, :] - target_coords[:, :, None]
    square_dist = jnp.sum(displace * displace, axis=0) + SOFTENING
    distance = jnp.sqrt(square_dist)
    cube_dist = square_dist * distance
    damped = THOLE_DAMP * cube_dist / jnp.sqrt(target_polar[:, None] * source_polar[None, :])
    damping = jnp.exp(-damped)
    tapering = jnp.square(jnp.maximum(1.0 - square_dist / CUTOFF_SQ, 0.0))
    keeper = (target_groups[:, None] != source_groups[None, :]).astype(jnp.float32)
    weight = tapering * keeper * target_occupied[:, None] * source_occupied[None, :]
    isotropic = weight * -jnp.expm1(-damped) / cube_dist
    tensorial = 3.0 * weight * (1.0 - (1.0 + damped) * damping) / (cube_dist * square_dist)
    return (displace, isotropic, tensorial)


def field_targets(displace, isotropic, tensorial, source_dipole):
    projected = jnp.sum(displace * source_dipole[:, None, :], axis=0)
    return jnp.sum(displace * (tensorial * projected)[None], axis=2) - jnp.sum(
        isotropic[None] * source_dipole[:, None, :], axis=2
    )


def field_sources(displace, isotropic, tensorial, target_dipole):
    projected = jnp.sum(displace * target_dipole[:, :, None], axis=0)
    return jnp.sum(displace * (tensorial * projected)[None], axis=1) - jnp.sum(
        isotropic[None] * target_dipole[:, :, None], axis=1
    )


def tiled(values, filler, tile_count):
    shaped = values.reshape(values.shape[:-1] + (tile_count, values.shape[-1] // tile_count))
    widths = [(0, 0)] * (shaped.ndim - 2) + [(1, 1), (0, 0)]
    return jnp.pad(shaped, widths, constant_values=filler)


def padded_coords(coords, tile_count):
    marker = tiled(jnp.zeros_like(coords), 1.0, tile_count)
    lifted = jnp.array([0.0, 0.0, FAR_LIFT], jnp.float32).reshape(3, 1, 1)
    return tiled(coords, 0.0, tile_count) + marker * lifted


def band_sources(padded, tile_at):
    coords, polarity, groups, occupied, dipole = padded

    def flat_vector(member):
        window_part = lax.dynamic_slice_in_dim(member, tile_at, 3, 2)
        return jnp.transpose(window_part, (1, 0, 2, 3)).reshape(3, -1)

    def flat_scalar(member):
        return lax.dynamic_slice_in_dim(member, tile_at, 3, 1).reshape(-1)

    return (
        flat_vector(coords),
        flat_scalar(polarity),
        flat_scalar(groups),
        flat_scalar(occupied),
        flat_vector(dipole),
    )


def target_tile(own_cell, first_slot, tile_width):
    coords, polarity, groups, occupied = own_cell
    return (
        lax.dynamic_slice_in_dim(coords, first_slot, tile_width, 1),
        lax.dynamic_slice_in_dim(polarity, first_slot, tile_width, 0),
        lax.dynamic_slice_in_dim(groups, first_slot, tile_width, 0),
        lax.dynamic_slice_in_dim(occupied, first_slot, tile_width, 0),
    )


def four_static(packed):
    east_cells = from_behind(packed, "gx", -1)
    next_own, next_east = from_behind((packed[0], east_cells[0]), "gy", -1)
    prior_east = from_behind(east_cells[-1], "gy", 1)
    north_cells = jnp.concatenate([packed[1:], next_own[None]], axis=0)
    north_east = jnp.concatenate([east_cells[1:], next_east[None]], axis=0)
    south_east = jnp.concatenate([prior_east[None], east_cells[:-1]], axis=0)
    return jnp.stack([east_cells, north_cells, north_east, south_east], axis=1)


def four_dipole(dipole):
    east_cells = from_behind(dipole, "gx", -1)
    next_own, next_east = from_behind((dipole[0], east_cells[0]), "gy", -1)
    prior_east = from_behind(east_cells[-1], "gy", 1)
    north_cells = jnp.concatenate([dipole[1:], next_own[None]], axis=0)
    north_east = jnp.concatenate([east_cells[1:], next_east[None]], axis=0)
    south_east = jnp.concatenate([prior_east[None], east_cells[:-1]], axis=0)
    return jnp.stack([east_cells, north_cells, north_east, south_east], axis=1)


def half_statics(coords, polarity, groups, occupied, tile_count):
    cell_count = coords.shape[0]
    packed = jnp.concatenate([coords, polarity[:, None], occupied[:, None]], axis=1)
    nearby = four_static(packed)
    lift_x = jnp.array(NEIGHBOUR_X, jnp.float32) * CELL_SIDE
    lift_y = jnp.array(NEIGHBOUR_Y, jnp.float32) * CELL_SIDE
    lifted = jnp.stack([lift_x, lift_y, jnp.zeros_like(lift_x)], axis=1)
    nearby_coords = nearby[:, :, 0:3] + lifted[None, :, :, None]
    nearby_groups = jnp.full((cell_count, 4, coords.shape[-1]), -1, jnp.int32)
    own_padded = (
        padded_coords(coords[:, None], tile_count),
        tiled(polarity[:, None], 1.0, tile_count),
        tiled(groups[:, None], -1, tile_count),
        tiled(occupied[:, None], 0.0, tile_count),
    )
    nearby_padded = (
        padded_coords(nearby_coords, tile_count),
        tiled(nearby[:, :, 3], 1.0, tile_count),
        tiled(nearby_groups, -1, tile_count),
        tiled(nearby[:, :, 4], 0.0, tile_count),
    )
    return (own_padded, nearby_padded)


def half_cell(own_cell, own_band, nearby_band, dipole, tile_count):
    tile_width = dipole.shape[-1] // tile_count

    def one_tile(tile_at, carry):
        own_field, back_field = carry
        first_slot = tile_at * tile_width
        target = target_tile(own_cell, first_slot, tile_width)
        target_dipole = lax.dynamic_slice_in_dim(dipole, first_slot, tile_width, 1)
        source = band_sources(own_band, tile_at)
        displace, isotropic, tensorial = pair_terms(
            target[0], target[1], target[2], target[3], source[0], source[1], source[2], source[3]
        )
        inside = field_targets(displace, isotropic, tensorial, source[4])
        source = band_sources(nearby_band, tile_at)
        displace, isotropic, tensorial = pair_terms(
            target[0], target[1], target[2], target[3], source[0], source[1], source[2], source[3]
        )
        outside = field_targets(displace, isotropic, tensorial, source[4])
        returned = field_sources(displace, isotropic, tensorial, target_dipole)
        returned = jnp.transpose(returned.reshape(3, 4, 3, tile_width), (1, 0, 2, 3))
        own_field = lax.dynamic_update_slice_in_dim(own_field, inside + outside, first_slot, 1)
        window = lax.dynamic_slice_in_dim(back_field, tile_at, 3, 2) + returned
        back_field = lax.dynamic_update_slice_in_dim(back_field, window, tile_at, 2)
        return (own_field, back_field)

    initial = (
        jnp.zeros(dipole.shape, jnp.float32),
        jnp.zeros((4, 3, tile_count + 2, tile_width), jnp.float32),
    )
    own_field, back_field = lax.fori_loop(0, tile_count, one_tile, initial)
    return (own_field, back_field[:, :, 1:-1].reshape(4, 3, -1))


def half_field(own_cells, statics, dipole, tile_count):
    own_padded, nearby_padded = statics
    own_band = own_padded + (tiled(dipole[:, None], 0.0, tile_count),)
    nearby_band = nearby_padded + (tiled(four_dipole(dipole), 0.0, tile_count),)

    def per_cell(members):
        return half_cell(members[0], members[1], members[2], members[3], tile_count)

    own_field, back_field = lax.map(per_cell, (own_cells, own_band, nearby_band, dipole))
    north_part = back_field[:, 1]
    north_east = back_field[:, 2]
    south_east = back_field[:, 3]
    from_below, below_east = from_behind((north_part[-1], north_east[-1]), "gy", 1)
    from_above = from_behind(south_east[0], "gy", -1)
    from_south = jnp.concatenate([from_below[None], north_part[:-1]], axis=0)
    from_south_west = jnp.concatenate([below_east[None], north_east[:-1]], axis=0)
    from_north = jnp.concatenate([south_east[1:], from_above[None]], axis=0)
    eastward = back_field[:, 0] + from_south_west + from_north
    from_west = from_behind(eastward, "gx", 1)
    return own_field + from_south + from_west


def diis_weights(gram_matrix):
    lower = jnp.linalg.cholesky(gram_matrix)
    history = gram_matrix.shape[0]
    forward = []
    for row_at in range(history):
        running = jnp.ones((), gram_matrix.dtype)
        for col_at in range(row_at):
            running = running - lower[row_at, col_at] * forward[col_at]
        forward.append(running / lower[row_at, row_at])
    backward = [None] * history
    for row_at in reversed(range(history)):
        running = forward[row_at]
        for col_at in range(row_at + 1, history):
            running = running - lower[col_at, row_at] * backward[col_at]
        backward[row_at] = running / lower[row_at, row_at]
    solved = jnp.stack(backward)
    return solved / jnp.sum(solved)


def body(
    positions, polarizability, tile_counts, molecules, perm_field, dipoles, past_out, past_res
):
    counts = tile_counts[0]
    cell_count = counts.shape[0]
    tile_count = counts.shape[1]
    coords = positions[0]
    atom_slots = coords.shape[-1]
    tile_width = atom_slots // tile_count
    slot_index = lax.broadcasted_iota(jnp.int32, (cell_count, tile_count, tile_width), 2)
    occupied = (slot_index < counts[:, :, None]).astype(jnp.float32).reshape(cell_count, atom_slots)
    polarity = polarizability[0]
    groups = molecules[0]
    own_cells = (coords, polarity, groups, occupied)
    occupied_vec = occupied[:, None, :]
    scaled = occupied_vec * polarity[:, None, :]
    stored_out = jnp.moveaxis(past_out[0], 1, 0) * occupied_vec
    stored_res = jnp.moveaxis(past_res[0], 1, 0) * occupied_vec
    current = dipoles[0] * occupied_vec
    permanent = perm_field[0]
    statics = half_statics(coords, polarity, groups, occupied, tile_count)
    weights = jnp.zeros((stored_out.shape[0] + 1,), jnp.float32)
    for step_at in range(ITERS):
        induced = half_field(own_cells, statics, current, tile_count)
        jacobi = scaled * (permanent + induced)
        residual = jacobi - current
        outputs_all = jnp.concatenate([stored_out, jacobi[None]], 0)
        residual_all = jnp.concatenate([stored_res, residual[None]], 0)
        flattened = residual_all.reshape(residual_all.shape[0], -1)
        local_gram = jnp.dot(
            flattened,
            flattened.T,
            precision=lax.Precision.HIGHEST,
            preferred_element_type=jnp.float32,
        )
        gram_matrix = lax.psum(local_gram, ("gx", "gy"))
        weights = diis_weights(gram_matrix)
        current = jnp.sum(weights[:, None, None, None] * outputs_all, axis=0)
        stored_out = outputs_all[1:]
        stored_res = residual_all[1:]
    return (current[None], weights)


def solution(mesh):
    placed = (
        P(("box", "gx"), "gy", None, None),
        P(("box", "gx"), "gy", None),
        P(("box", "gx"), "gy", None),
        P(("box", "gx"), "gy", None),
        P(("box", "gx"), "gy", None, None),
        P(("box", "gx"), "gy", None, None),
        P(("box", "gx"), "gy", None, None, None),
        P(("box", "gx"), "gy", None, None, None),
    )
    return jax.shard_map(
        body,
        mesh=mesh,
        in_specs=placed,
        out_specs=(P(("box", "gx"), "gy", None, None), P("box")),
        check_vma=False,
    )
```

profile of v0, /device:TPU:0, one launch (start us, length us, event | category | flops | bytes accessed | tf_op | source)
XLA Modules:
  0.0 246.8 jit_solution(973416661079791287)
XLA Ops:
  0.7 0.8 broadcast_bitcast_fusion
  1.4 0.7 bitcast_multiply_fusion.2
  2.1 6.0 %collective-permute-start.4 = (f32[2,3,256]{2,1,0:T(4,128)S(1)}, f32[2,3,256]{2,1,0:T(4,128)S(1)}, u32[]{:S(2)}, u32[]{:S(2)}) collective-permute-start(f32[2,3,256]{2,1,0:T(4,128)S(1)} %bitcast_multiply_fusion.2), channel_id=1, source_target_pairs={{2,0},{4,2},{6,4},{8,6},{10,8},{12,10},{14,12},{0,14},{3,1},{5,3},... | collective-permute-start | bytes 18440 | tf_op jit(solution)/shard_map/ppermute | solution.py:19
  8.2 0.7 lt.120
  8.9 0.7 broadcast_in_dim_squeeze.8
  9.6 0.7 copy.384
  11.1 0.8 iota_compare_fusion.4
  11.9 0.8 compare_convert_fusion.1
  12.6 0.7 copy.283
  13.3 0.7 copy.284
  14.1 0.7 pad_bitcast_fusion
  14.8 0.7 reshape_broadcast_in_dim_squeeze.10
  15.6 0.7 reshape_broadcast_in_dim_squeeze.11
  20.0 23.1 %while.55 = (s32[]{:T(128)}, f32[2,3,256]{2,1,0:T(4,128)S(1)}, f32[2,4,3,256]{3,1,2,0:T(4,128)S(1)}, f32[2,3,256]{2,1,0:T(4,128)S(1)}, f32[2,256]{1,0:T(2,128)S(...) while((s32[]{:T(128)}, f32[2,3,256]{2,1,0:T(4,128)S(1)}, ...), condition=%wide.region_14.15_spmd, body=%wide.region_0.14_spmd.sunk | while | flops 19906180 | bytes 14344956 | solution.py:186
  20.2 11.3 %while.58 = (s32[]{:T(128)}, f32[3,256]{1,0:T(4,128)S(1)}, f32[4,3,4,128]{3,2,0,1:T(4,128)S(1)}, f32[1,3,4,128]{3,2,1,0:T(4,128)S(1)}, f32[3,256]{1,0:T(4,128)S(...) while((s32[]{:T(128)}, f32[3,256]{1,0:T(4,128)S(1)}, ...), condition=%wide.region_13.13_spmd, body=%wide.region_1.12_spmd.sunk | while | flops 19906180 | bytes 14031151 | solution.py:174
  21.9 1.0 fusion.153
  22.8 1.0 fusion.154
  23.8 1.0 fusion.155
  24.9 0.6 fusion.156
  27.5 1.0 fusion.153
  28.5 1.0 fusion.154
  29.5 1.0 fusion.155
  30.6 0.6 fusion.156
  31.7 11.3 %while.58 = (s32[]{:T(128)}, f32[3,256]{1,0:T(4,128)S(1)}, f32[4,3,4,128]{3,2,0,1:T(4,128)S(1)}, f32[1,3,4,128]{3,2,1,0:T(4,128)S(1)}, f32[3,256]{1,0:T(4,128)S(...) while((s32[]{:T(128)}, f32[3,256]{1,0:T(4,128)S(1)}, ...), condition=%wide.region_13.13_spmd, body=%wide.region_1.12_spmd.sunk | while | flops 19906180 | bytes 14031151 | solution.py:174
  33.4 1.0 fusion.153
  34.4 1.0 fusion.154
  35.4 1.0 fusion.155
  36.5 0.6 fusion.156
  39.0 1.0 fusion.153
  40.0 1.0 fusion.154
  41.0 1.0 fusion.155
  42.1 0.6 fusion.156
  44.7 1.5 collective-permute-start.11
  46.2 4.8 %collective-permute-done.11 = f32[2,3,256]{2,1,0:T(4,128)S(1)} collective-permute-done((f32[2,3,256]{2,1,0:T(4,128)S(1)}, f32[2,3,256]{2,1,0:T(4,128)S(1)}, u32[]{:S(2)}, u32[]{:S(2)}) %collective-permute-start.11) | collective-permute-done | bytes 6176 | tf_op jit(solution)/shard_map/ppermute | solution.py:19
  51.3 29.5 %psum.14 = f32[8,8]{0,1:T(8,128)S(1)} all-reduce(f32[8,8]{0,1:T(8,128)S(1)} %convolution_bitcast_fusion.1), channel_id=1, replica_groups=mesh['box'=2,'gx'=8,'gy'=2] {'gx','gy'}, use_global_device_ids=true, to_apply=%region_15.16 | all-reduce | flops 64 | bytes 512 | tf_op jit(solution)/shard_map/psum | solution.py:254
  80.9 0.7 cholesky.44
  81.6 0.6 compare_reduce_fusion.1
  82.3 0.6 fusion.88
  82.9 0.7 fusion.107
  83.6 0.7 fusion.106
  130.7 3.5 %collective-permute-done.12 = f32[2,3,256]{2,1,0:T(4,128)S(1)} collective-permute-done((f32[2,3,256]{2,1,0:T(4,128)S(1)}, f32[2,3,256]{2,1,0:T(4,128)S(1)}, u32[]{:S(2)}, u32[]{:S(2)}) %collective-permute-start.12) | collective-permute-done | bytes 6176 | tf_op jit(solution)/shard_map/ppermute | solution.py:19
  135.7 23.1 %while.57 = (s32[]{:T(128)}, f32[2,3,256]{2,1,0:T(4,128)S(1)}, f32[2,4,3,256]{3,1,2,0:T(4,128)S(1)}, f32[2,3,256]{2,1,0:T(4,128)S(1)}, f32[2,256]{1,0:T(2,128)S(...) while((s32[]{:T(128)}, f32[2,3,256]{2,1,0:T(4,128)S(1)}, ...), condition=%wide.region_33.35_spmd, body=%wide.region_19.34_spmd.sunk | while | flops 19906180 | bytes 14344960 | solution.py:186
  135.9 11.3 %while.59 = (s32[]{:T(128)}, f32[3,256]{1,0:T(4,128)S(1)}, f32[4,3,4,128]{3,2,0,1:T(4,128)S(1)}, f32[1,3,4,128]{3,2,1,0:T(4,128)S(1)}, f32[3,256]{1,0:T(4,128)S(...) while((s32[]{:T(128)}, f32[3,256]{1,0:T(4,128)S(1)}, ...), condition=%wide.region_32.33_spmd, body=%wide.region_20.32_spmd.sunk | while | flops 19906180 | bytes 14031151 | solution.py:174
  137.6 1.0 fusion.143
  138.6 1.0 fusion.144
  139.6 1.0 fusion.145
  143.2 1.0 fusion.143
  144.2 1.0 fusion.144
  145.2 1.0 fusion.145
  146.3 0.6 fusion.146
  147.5 11.3 %while.59 = (s32[]{:T(128)}, f32[3,256]{1,0:T(4,128)S(1)}, f32[4,3,4,128]{3,2,0,1:T(4,128)S(1)}, f32[1,3,4,128]{3,2,1,0:T(4,128)S(1)}, f32[3,256]{1,0:T(4,128)S(...) while((s32[]{:T(128)}, f32[3,256]{1,0:T(4,128)S(1)}, ...), condition=%wide.region_32.33_spmd, body=%wide.region_20.32_spmd.sunk | while | flops 19906180 | bytes 14031151 | solution.py:174
  149.2 1.0 fusion.143
  150.2 1.0 fusion.144
  151.2 1.0 fusion.145
  154.8 1.0 fusion.143
  155.8 1.0 fusion.144
  156.8 1.0 fusion.145
  160.7 6.1 %collective-permute-done.19 = f32[2,3,256]{2,1,0:T(4,128)S(1)} collective-permute-done((f32[2,3,256]{2,1,0:T(4,128)S(1)}, f32[2,3,256]{2,1,0:T(4,128)S(1)}, u32[]{:S(2)}, u32[]{:S(2)}) %collective-permute-start.19) | collective-permute-done | bytes 6176 | tf_op jit(solution)/shard_map/ppermute | solution.py:19
  167.1 29.5 %psum.15 = f32[8,8]{0,1:T(8,128)S(1)} all-reduce(f32[8,8]{0,1:T(8,128)S(1)} %convolution_bitcast_fusion), channel_id=1, replica_groups=mesh['box'=2,'gx'=8,'gy'=2] {'gx','gy'}, use_global_device_ids=true, to_apply=%region_34.36 | all-reduce | flops 64 | bytes 512 | tf_op jit(solution)/shard_map/psum | solution.py:254
  196.7 0.7 cholesky.55
  197.4 0.6 compare_reduce_fusion
  198.1 0.6 select_select_fusion
  198.7 0.7 fusion.105
  199.4 0.7 fusion.104
  (432 shorter events, 29.0 us)
Async XLA Ops:
  0.6 19.1 %copy-start.6 = (f32[3]{0:T(128)S(1)}, f32[3]{0:T(128)}, u32[]{:S(2)}) copy-start(f32[3]{0:T(128)} %constant.290.clone) | copy-start | bytes 40
  0.6 18.9 %copy-start.7 = (f32[4,3]{1,0:T(4,128)S(1)}, f32[4,3]{1,0:T(4,128)}, u32[]{:S(2)}) copy-start(f32[4,3]{1,0:T(4,128)} %constant.329) | copy-start | bytes 148
  0.7 19.3 %copy-start = (f32[1,2,256]{2,1,0:T(2,128)S(1)}, f32[1,2,256]{2,1,0:T(2,128)}, u32[]{:S(2)}) copy-start(f32[1,2,256]{2,1,0:T(2,128)} %param.22) | copy-start | bytes 6148
  0.7 19.3 %copy-start.1 = (s32[1,2,256]{2,1,0:T(2,128)S(1)}, s32[1,2,256]{2,1,0:T(2,128)}, u32[]{:S(2)}) copy-start(s32[1,2,256]{2,1,0:T(2,128)} %param.24) | copy-start | bytes 6148
  2.1 14.2 %collective-permute-start.4 = (f32[2,3,256]{2,1,0:T(4,128)S(1)}, f32[2,3,256]{2,1,0:T(4,128)S(1)}, u32[]{:S(2)}, u32[]{:S(2)}) collective-permute-start(f32[2,3,256]{2,1,0:T(4,128)S(1)} %bitcast_multiply_fusion.2), channel_id=1, source_target_pairs={{2,0},{4,2},{6,4},{8,6},{10,8},{12,10},{14,12},{0,14},{3,1},{5,3},... | collective-permute-start | bytes 18440 | tf_op jit(solution)/shard_map/ppermute | solution.py:19
  8.2 8.2 %collective-permute-start.5 = (f32[3,256]{1,0:T(4,128)S(1)}, f32[3,256]{1,0:T(4,128)S(1)}, u32[]{:S(2)}, u32[]{:S(2)}) collective-permute-start(f32[3,256]{1,0:T(4,128)S(1)} %get-tuple-element.1237), channel_id=1, source_target_pairs={{1,0},{0,1},{3,2},{2,3},{5,4},{4,5},{7,6},{6,7},{9,8},{8,9},{11,10... | collective-permute-start | bytes 9224 | tf_op jit(solution)/shard_map/ppermute | solution.py:19
  10.3 7.6 %collective-permute-start = (f32[2,5,256]{2,1,0:T(8,128)S(1)}, f32[2,5,256]{2,1,0:T(8,128)S(1)}, u32[]{:S(2)}, u32[]{:S(2)}) collective-permute-start(f32[2,5,256]{2,1,0:T(8,128)S(1)} %pad_maximum_fusion.4), channel_id=1, source_target_pairs={{2,0},{4,2},{6,4},{8,6},{10,8},{12,10},{14,12},{0,14},{3,1},{5,3},... | collective-permute-start | bytes 30728 | tf_op jit(solution)/shard_map/ppermute | solution.py:19
  10.9 6.1 %collective-permute-start.1 = (f32[5,256]{1,0:T(8,128)S(1)}, f32[5,256]{1,0:T(8,128)S(1)}, u32[]{:S(2)}, u32[]{:S(2)}) collective-permute-start(f32[5,256]{1,0:T(8,128)S(1)} %get-tuple-element.1225), channel_id=1, source_target_pairs={{1,0},{0,1},{3,2},{2,3},{5,4},{4,5},{7,6},{6,7},{9,8},{8,9},{11,10... | collective-permute-start | bytes 15368 | tf_op jit(solution)/shard_map/ppermute | solution.py:19
  16.4 1.2 collective-permute-start.7
  16.7 1.2 collective-permute-start.6
  17.9 1.2 collective-permute-start.3
  18.3 1.2 collective-permute-start.2
  19.9 23.8 %copy-start.3 = (f32[1,2,7,3,256]{4,1,3,2,0:T(2,128)S(1)}, f32[1,2,7,3,256]{4,1,3,2,0:T(2,128)}, u32[]{:S(2)}) copy-start(f32[1,2,7,3,256]{4,1,3,2,0:T(2,128)} %param.28) | copy-start | bytes 129028
  19.9 23.8 %copy-start.4 = (f32[1,2,7,3,256]{4,1,3,2,0:T(2,128)S(1)}, f32[1,2,7,3,256]{4,1,3,2,0:T(2,128)}, u32[]{:S(2)}) copy-start(f32[1,2,7,3,256]{4,1,3,2,0:T(2,128)} %param.27) | copy-start | bytes 129028
  19.9 31.1 %copy-start.2 = (f32[1,2,3,256]{3,1,2,0:T(2,128)S(1)}, f32[1,2,3,256]{3,1,2,0:T(2,128)}, u32[]{:S(2)}) copy-start(f32[1,2,3,256]{3,1,2,0:T(2,128)} %param.26) | copy-start | bytes 18436
  20.0 31.1 %copy-start.5 = (f32[1,2,3,256]{3,1,2,0:T(2,128)S(1)}, f32[1,2,3,256]{3,1,2,0:T(2,128)}, u32[]{:S(2)}) copy-start(f32[1,2,3,256]{3,1,2,0:T(2,128)} %param.25) | copy-start | bytes 18436
  43.1 1.2 collective-permute-start.10
  43.5 1.2 collective-permute-start.9
  43.7 2.5 collective-permute-start.8
  44.7 6.4 %collective-permute-start.11 = (f32[2,3,256]{2,1,0:T(4,128)S(1)}, f32[2,3,256]{2,1,0:T(4,128)S(1)}, u32[]{:S(2)}, u32[]{:S(2)}) collective-permute-start(f32[2,3,256]{2,1,0:T(4,128)S(1)} %fusion.77), channel_id=1, source_target_pairs={{14,0},{0,2},{2,4},{4,6},{6,8},{8,10},{10,12},{12,14},{15,1},{1,3}... | collective-permute-start | bytes 18440 | tf_op jit(solution)/shard_map/ppermute | solution.py:19
  130.4 3.9 %collective-permute-start.12 = (f32[2,3,256]{2,1,0:T(4,128)S(1)}, f32[2,3,256]{2,1,0:T(4,128)S(1)}, u32[]{:S(2)}, u32[]{:S(2)}) collective-permute-start(f32[2,3,256]{2,1,0:T(4,128)S(1)} %fusion.59), channel_id=1, source_target_pairs={{2,0},{4,2},{6,4},{8,6},{10,8},{12,10},{14,12},{0,14},{3,1},{5,3},... | collective-permute-start | bytes 18440 | tf_op jit(solution)/shard_map/ppermute | solution.py:19
  130.7 4.2 %collective-permute-start.13 = (f32[3,256]{1,0:T(4,128)S(1)}, f32[3,256]{1,0:T(4,128)S(1)}, u32[]{:S(2)}, u32[]{:S(2)}) collective-permute-start(f32[3,256]{1,0:T(4,128)S(1)} %get-tuple-element.1231), channel_id=1, source_target_pairs={{1,0},{0,1},{3,2},{2,3},{5,4},{4,5},{7,6},{6,7},{9,8},{8,9},{11,10... | collective-permute-start | bytes 9224 | tf_op jit(solution)/shard_map/ppermute | solution.py:19
  134.3 1.2 collective-permute-start.15
  134.3 1.3 collective-permute-start.14
  158.9 1.2 collective-permute-start.18
  159.3 1.2 collective-permute-start.17
  159.5 1.2 collective-permute-start.16
  160.5 6.4 %collective-permute-start.19 = (f32[2,3,256]{2,1,0:T(4,128)S(1)}, f32[2,3,256]{2,1,0:T(4,128)S(1)}, u32[]{:S(2)}, u32[]{:S(2)}) collective-permute-start(f32[2,3,256]{2,1,0:T(4,128)S(1)} %fusion.75), channel_id=1, source_target_pairs={{14,0},{0,2},{2,4},{4,6},{6,8},{8,10},{10,12},{12,14},{15,1},{1,3}... | collective-permute-start | bytes 18440 | tf_op jit(solution)/shard_map/ppermute | solution.py:19
  246.1 0.7 copy-start.8
where the time goes:
time: 249 us; the launch traced here: 247 us
  between operations  92.8 us (37%)
  blocking collectives  59 us (24%)
  other arithmetic  47 us (19%)
  waiting for transfers between devices  18.3 us (7%)
  local copies, waits for them, and re-layouts  15.3 us (6%)
  starting transfers between devices  12.4 us (5%)
    psum x2, blocking collectives, body(): gram_matrix = lax.psum(local_gram, ('gx', 'gy'))  59 us
    ppermute x20, waiting for transfers between devices, from_behind(): return lax.ppermute(block, axis, route)  18.3 us
    ppermute x20, starting transfers between devices, from_behind(): return lax.ppermute(block, axis, route)  12.4 us
    div x16, other arithmetic, pair_terms(): isotropic = weight * -jnp.expm1(-damped) / cube_dist  10.8 us
    reduce_sum x8, other arithmetic, field_sources(): projected = jnp.sum(displace * target_dipole[:, :, None], axis=0)  8.01 us
    mul x8, other arithmetic, field_targets(): tensorial * projected  7.77 us
    reduce_sum x8, other arithmetic, field_sources(): jnp.sum(displace * (tensorial * projected)[None], axis=1)  5.08 us
  transfers between devices with their start and end apart: 20, of which 14 were waited for; matrix products, arithmetic and copies ran while one was open for 3% of the time, Pallas kernels for 0%

commit v1 on v0

--- a/solution.py
+++ b/solution.py
@@ -251,7 +251,7 @@
             precision=lax.Precision.HIGHEST,
             preferred_element_type=jnp.float32,
         )
-        gram_matrix = lax.psum(local_gram, ("gx", "gy"))
+        gram_matrix = lax.psum(lax.psum(local_gram, "gy"), "gx")
         weights = diis_weights(gram_matrix)
         current = jnp.sum(weights[:, None, None, None] * outputs_all, axis=0)
         stored_out = outputs_all[1:]

time: 249 us -> 231 us (0.928)
  blocking collectives: 59 us -> 41.2 us
  waiting for transfers between devices: 18.3 us -> 13.5 us
  starting transfers between devices: 12.4 us -> 17.2 us
    psum x2 -> x4, blocking collectives: 59 us -> 41.2 us  [body(): gram_matrix = lax.psum(lax.psum(local_gram, 'gy'), 'gx')]
    ppermute x20, starting transfers between devices: 12.4 us -> 17.2 us  [from_behind(): return lax.ppermute(block, axis, route)]
    ppermute x20, waiting for transfers between devices: 18.3 us -> 13.5 us  [from_behind(): return lax.ppermute(block, axis, route)]
  transfers between devices with their start and end apart: 20 -> 20, of which waited for: 14 -> 13; matrix products, arithmetic and copies ran while one was open for 3% -> 3% of each run, Pallas kernels for 0% -> 0%
where the time goes in v1:
time: 231 us; the launch traced here: 229 us
  between operations  92.8 us (40%)
  other arithmetic  47 us (20%)
  blocking collectives  41.2 us (18%)
  starting transfers between devices  17.2 us (7%)
  local copies, waits for them, and re-layouts  15.3 us (7%)
  waiting for transfers between devices  13.5 us (6%)
    psum x4, blocking collectives, body(): gram_matrix = lax.psum(lax.psum(local_gram, 'gy'), 'gx')  41.2 us
    ppermute x20, starting transfers between devices, from_behind(): return lax.ppermute(block, axis, route)  17.2 us
    ppermute x20, waiting for transfers between devices, from_behind(): return lax.ppermute(block, axis, route)  13.5 us
    div x16, other arithmetic, pair_terms(): isotropic = weight * -jnp.expm1(-damped) / cube_dist  10.8 us
    reduce_sum x8, other arithmetic, field_sources(): projected = jnp.sum(displace * target_dipole[:, :, None], axis=0)  8.01 us
    mul x8, other arithmetic, field_targets(): tensorial * projected  7.77 us
    reduce_sum x8, other arithmetic, field_sources(): jnp.sum(displace * (tensorial * projected)[None], axis=1)  5.08 us
  transfers between devices with their start and end apart: 20, of which 13 were waited for; matrix products, arithmetic and copies ran while one was open for 3% of the time, Pallas kernels for 0%

profile of v1, /device:TPU:0, one launch (start us, length us, event | category | flops | bytes accessed | tf_op | source)
XLA Modules:
  0.0 229.0 jit_solution(10589178224206303825)
XLA Ops:
  0.7 0.8 broadcast_bitcast_fusion
  1.4 0.7 bitcast_multiply_fusion.2
  2.1 6.0 %collective-permute-start.4 = (f32[2,3,256]{2,1,0:T(4,128)S(1)}, f32[2,3,256]{2,1,0:T(4,128)S(1)}, u32[]{:S(2)}, u32[]{:S(2)}) collective-permute-start(f32[2,3,256]{2,1,0:T(4,128)S(1)} %bitcast_multiply_fusion.2), channel_id=1, source_target_pairs={{2,0},{4,2},{6,4},{8,6},{10,8},{12,10},{14,12},{0,14},{3,1},{5,3},... | collective-permute-start | bytes 18440 | tf_op jit(solution)/shard_map/ppermute | solution.py:19
  8.2 0.7 lt.120
  8.9 0.7 broadcast_in_dim_squeeze.8
  9.6 0.7 copy.384
  11.1 0.8 iota_compare_fusion.4
  11.9 0.8 compare_convert_fusion.1
  12.6 0.7 copy.283
  13.3 0.7 copy.284
  14.1 0.7 pad_bitcast_fusion
  14.8 0.7 reshape_broadcast_in_dim_squeeze.10
  15.6 0.7 reshape_broadcast_in_dim_squeeze.11
  20.0 23.1 %while.55 = (s32[]{:T(128)}, f32[2,3,256]{2,1,0:T(4,128)S(1)}, f32[2,4,3,256]{3,1,2,0:T(4,128)S(1)}, f32[2,3,256]{2,1,0:T(4,128)S(1)}, f32[2,256]{1,0:T(2,128)S(...) while((s32[]{:T(128)}, f32[2,3,256]{2,1,0:T(4,128)S(1)}, ...), condition=%wide.region_14.15_spmd, body=%wide.region_0.14_spmd.sunk | while | flops 19906180 | bytes 14344956 | solution.py:186
  20.2 11.3 %while.58 = (s32[]{:T(128)}, f32[3,256]{1,0:T(4,128)S(1)}, f32[4,3,4,128]{3,2,0,1:T(4,128)S(1)}, f32[1,3,4,128]{3,2,1,0:T(4,128)S(1)}, f32[3,256]{1,0:T(4,128)S(...) while((s32[]{:T(128)}, f32[3,256]{1,0:T(4,128)S(1)}, ...), condition=%wide.region_13.13_spmd, body=%wide.region_1.12_spmd.sunk | while | flops 19906180 | bytes 14031151 | solution.py:174
  21.9 1.0 fusion.153
  22.8 1.0 fusion.154
  23.8 1.0 fusion.155
  24.9 0.6 fusion.156
  27.5 1.0 fusion.153
  28.5 1.0 fusion.154
  29.5 1.0 fusion.155
  31.7 11.3 %while.58 = (s32[]{:T(128)}, f32[3,256]{1,0:T(4,128)S(1)}, f32[4,3,4,128]{3,2,0,1:T(4,128)S(1)}, f32[1,3,4,128]{3,2,1,0:T(4,128)S(1)}, f32[3,256]{1,0:T(4,128)S(...) while((s32[]{:T(128)}, f32[3,256]{1,0:T(4,128)S(1)}, ...), condition=%wide.region_13.13_spmd, body=%wide.region_1.12_spmd.sunk | while | flops 19906180 | bytes 14031151 | solution.py:174
  33.4 1.0 fusion.153
  34.4 1.0 fusion.154
  35.4 1.0 fusion.155
  39.0 1.0 fusion.153
  40.0 1.0 fusion.154
  41.0 1.0 fusion.155
  44.7 1.5 collective-permute-start.11
  46.2 4.8 %collective-permute-done.11 = f32[2,3,256]{2,1,0:T(4,128)S(1)} collective-permute-done((f32[2,3,256]{2,1,0:T(4,128)S(1)}, f32[2,3,256]{2,1,0:T(4,128)S(1)}, u32[]{:S(2)}, u32[]{:S(2)}) %collective-permute-start.11) | collective-permute-done | bytes 6176 | tf_op jit(solution)/shard_map/ppermute | solution.py:19
  51.3 2.5 %psum.28 = f32[8,8]{0,1:T(8,128)S(1)} all-reduce(f32[8,8]{0,1:T(8,128)S(1)} %convolution_bitcast_fusion.1), channel_id=1, replica_groups=mesh['box'=2,'gx'=8,'gy'=2] {'gy'}, use_global_device_ids=true, to_apply=%region_15.16 | all-reduce | flops 64 | bytes 512 | tf_op jit(solution)/shard_map/psum | solution.py:254
  53.8 17.1 %psum.29 = f32[8,8]{0,1:T(8,128)S(1)} all-reduce(f32[8,8]{0,1:T(8,128)S(1)} %psum.28), channel_id=1, replica_groups=mesh['box'=2,'gx'=8,'gy'=2] {'gx'}, use_global_device_ids=true, to_apply=%region_16.17 | all-reduce | flops 64 | bytes 512 | tf_op jit(solution)/shard_map/psum | solution.py:254
  71.0 0.7 cholesky.44
  71.7 0.6 compare_reduce_fusion.1
  72.3 0.6 fusion.88
  73.0 0.7 fusion.107
  73.7 0.7 fusion.106
  120.5 2.2 collective-permute-start.12
  122.7 1.6 collective-permute-done.12
  125.8 23.1 %while.57 = (s32[]{:T(128)}, f32[2,3,256]{2,1,0:T(4,128)S(1)}, f32[2,4,3,256]{3,1,2,0:T(4,128)S(1)}, f32[2,3,256]{2,1,0:T(4,128)S(1)}, f32[2,256]{1,0:T(2,128)S(...) while((s32[]{:T(128)}, f32[2,3,256]{2,1,0:T(4,128)S(1)}, ...), condition=%wide.region_34.36_spmd, body=%wide.region_20.35_spmd.sunk | while | flops 19906180 | bytes 14344960 | solution.py:186
  126.0 11.3 %while.59 = (s32[]{:T(128)}, f32[3,256]{1,0:T(4,128)S(1)}, f32[4,3,4,128]{3,2,0,1:T(4,128)S(1)}, f32[1,3,4,128]{3,2,1,0:T(4,128)S(1)}, f32[3,256]{1,0:T(4,128)S(...) while((s32[]{:T(128)}, f32[3,256]{1,0:T(4,128)S(1)}, ...), condition=%wide.region_33.34_spmd, body=%wide.region_21.33_spmd.sunk | while | flops 19906180 | bytes 14031151 | solution.py:174
  127.7 1.0 fusion.143
  128.7 1.0 fusion.144
  129.7 1.0 fusion.145
  133.3 1.0 fusion.143
  134.3 1.0 fusion.144
  135.3 1.0 fusion.145
  137.6 11.3 %while.59 = (s32[]{:T(128)}, f32[3,256]{1,0:T(4,128)S(1)}, f32[4,3,4,128]{3,2,0,1:T(4,128)S(1)}, f32[1,3,4,128]{3,2,1,0:T(4,128)S(1)}, f32[3,256]{1,0:T(4,128)S(...) while((s32[]{:T(128)}, f32[3,256]{1,0:T(4,128)S(1)}, ...), condition=%wide.region_33.34_spmd, body=%wide.region_21.33_spmd.sunk | while | flops 19906180 | bytes 14031151 | solution.py:174
  139.3 1.0 fusion.143
  140.2 1.0 fusion.144
  141.3 1.0 fusion.145
  144.9 1.0 fusion.143
  145.9 1.0 fusion.144
  146.9 1.0 fusion.145
  150.6 3.0 %collective-permute-start.19 = (f32[2,3,256]{2,1,0:T(4,128)S(1)}, f32[2,3,256]{2,1,0:T(4,128)S(1)}, u32[]{:S(2)}, u32[]{:S(2)}) collective-permute-start(f32[2,3,256]{2,1,0:T(4,128)S(1)} %fusion.75), channel_id=1, source_target_pairs={{14,0},{0,2},{2,4},{4,6},{6,8},{8,10},{10,12},{12,14},{15,1},{1,3}... | collective-permute-start | bytes 18440 | tf_op jit(solution)/shard_map/ppermute | solution.py:19
  153.6 3.4 %collective-permute-done.19 = f32[2,3,256]{2,1,0:T(4,128)S(1)} collective-permute-done((f32[2,3,256]{2,1,0:T(4,128)S(1)}, f32[2,3,256]{2,1,0:T(4,128)S(1)}, u32[]{:S(2)}, u32[]{:S(2)}) %collective-permute-start.19) | collective-permute-done | bytes 6176 | tf_op jit(solution)/shard_map/ppermute | solution.py:19
  157.2 2.5 %psum.30 = f32[8,8]{0,1:T(8,128)S(1)} all-reduce(f32[8,8]{0,1:T(8,128)S(1)} %convolution_bitcast_fusion), channel_id=1, replica_groups=mesh['box'=2,'gx'=8,'gy'=2] {'gy'}, use_global_device_ids=true, to_apply=%region_35.37 | all-reduce | flops 64 | bytes 512 | tf_op jit(solution)/shard_map/psum | solution.py:254
  159.7 19.1 %psum.31 = f32[8,8]{0,1:T(8,128)S(1)} all-reduce(f32[8,8]{0,1:T(8,128)S(1)} %psum.30), channel_id=1, replica_groups=mesh['box'=2,'gx'=8,'gy'=2] {'gx'}, use_global_device_ids=true, to_apply=%region_36.38 | all-reduce | flops 64 | bytes 512 | tf_op jit(solution)/shard_map/psum | solution.py:254
  178.9 0.7 cholesky.55
  179.6 0.6 compare_reduce_fusion
  180.3 0.6 select_select_fusion
  180.9 0.7 fusion.105
  181.6 0.7 fusion.104
  (434 shorter events, 31.0 us)
Async XLA Ops:
  0.6 19.1 %copy-start.6 = (f32[3]{0:T(128)S(1)}, f32[3]{0:T(128)}, u32[]{:S(2)}) copy-start(f32[3]{0:T(128)} %constant.290.clone) | copy-start | bytes 40
  0.6 18.9 %copy-start.7 = (f32[4,3]{1,0:T(4,128)S(1)}, f32[4,3]{1,0:T(4,128)}, u32[]{:S(2)}) copy-start(f32[4,3]{1,0:T(4,128)} %constant.329) | copy-start | bytes 148
  0.7 19.3 %copy-start = (f32[1,2,256]{2,1,0:T(2,128)S(1)}, f32[1,2,256]{2,1,0:T(2,128)}, u32[]{:S(2)}) copy-start(f32[1,2,256]{2,1,0:T(2,128)} %param.22) | copy-start | bytes 6148
  0.7 19.3 %copy-start.1 = (s32[1,2,256]{2,1,0:T(2,128)S(1)}, s32[1,2,256]{2,1,0:T(2,128)}, u32[]{:S(2)}) copy-start(s32[1,2,256]{2,1,0:T(2,128)} %param.24) | copy-start | bytes 6148
  2.1 14.2 %collective-permute-start.4 = (f32[2,3,256]{2,1,0:T(4,128)S(1)}, f32[2,3,256]{2,1,0:T(4,128)S(1)}, u32[]{:S(2)}, u32[]{:S(2)}) collective-permute-start(f32[2,3,256]{2,1,0:T(4,128)S(1)} %bitcast_multiply_fusion.2), channel_id=1, source_target_pairs={{2,0},{4,2},{6,4},{8,6},{10,8},{12,10},{14,12},{0,14},{3,1},{5,3},... | collective-permute-start | bytes 18440 | tf_op jit(solution)/shard_map/ppermute | solution.py:19
  8.2 8.2 %collective-permute-start.5 = (f32[3,256]{1,0:T(4,128)S(1)}, f32[3,256]{1,0:T(4,128)S(1)}, u32[]{:S(2)}, u32[]{:S(2)}) collective-permute-start(f32[3,256]{1,0:T(4,128)S(1)} %get-tuple-element.1237), channel_id=1, source_target_pairs={{1,0},{0,1},{3,2},{2,3},{5,4},{4,5},{7,6},{6,7},{9,8},{8,9},{11,10... | collective-permute-start | bytes 9224 | tf_op jit(solution)/shard_map/ppermute | solution.py:19
  10.3 7.6 %collective-permute-start = (f32[2,5,256]{2,1,0:T(8,128)S(1)}, f32[2,5,256]{2,1,0:T(8,128)S(1)}, u32[]{:S(2)}, u32[]{:S(2)}) collective-permute-start(f32[2,5,256]{2,1,0:T(8,128)S(1)} %pad_maximum_fusion.4), channel_id=1, source_target_pairs={{2,0},{4,2},{6,4},{8,6},{10,8},{12,10},{14,12},{0,14},{3,1},{5,3},... | collective-permute-start | bytes 30728 | tf_op jit(solution)/shard_map/ppermute | solution.py:19
  10.9 6.1 %collective-permute-start.1 = (f32[5,256]{1,0:T(8,128)S(1)}, f32[5,256]{1,0:T(8,128)S(1)}, u32[]{:S(2)}, u32[]{:S(2)}) collective-permute-start(f32[5,256]{1,0:T(8,128)S(1)} %get-tuple-element.1225), channel_id=1, source_target_pairs={{1,0},{0,1},{3,2},{2,3},{5,4},{4,5},{7,6},{6,7},{9,8},{8,9},{11,10... | collective-permute-start | bytes 15368 | tf_op jit(solution)/shard_map/ppermute | solution.py:19
  16.4 1.2 collective-permute-start.7
  16.7 1.2 collective-permute-start.6
  17.9 1.2 collective-permute-start.3
  18.3 1.2 collective-permute-start.2
  19.9 23.8 %copy-start.3 = (f32[1,2,7,3,256]{4,1,3,2,0:T(2,128)S(1)}, f32[1,2,7,3,256]{4,1,3,2,0:T(2,128)}, u32[]{:S(2)}) copy-start(f32[1,2,7,3,256]{4,1,3,2,0:T(2,128)} %param.28) | copy-start | bytes 129028
  19.9 23.8 %copy-start.4 = (f32[1,2,7,3,256]{4,1,3,2,0:T(2,128)S(1)}, f32[1,2,7,3,256]{4,1,3,2,0:T(2,128)}, u32[]{:S(2)}) copy-start(f32[1,2,7,3,256]{4,1,3,2,0:T(2,128)} %param.27) | copy-start | bytes 129028
  19.9 31.1 %copy-start.2 = (f32[1,2,3,256]{3,1,2,0:T(2,128)S(1)}, f32[1,2,3,256]{3,1,2,0:T(2,128)}, u32[]{:S(2)}) copy-start(f32[1,2,3,256]{3,1,2,0:T(2,128)} %param.26) | copy-start | bytes 18436
  20.0 31.1 %copy-start.5 = (f32[1,2,3,256]{3,1,2,0:T(2,128)S(1)}, f32[1,2,3,256]{3,1,2,0:T(2,128)}, u32[]{:S(2)}) copy-start(f32[1,2,3,256]{3,1,2,0:T(2,128)} %param.25) | copy-start | bytes 18436
  43.1 1.2 collective-permute-start.10
  43.5 1.2 collective-permute-start.9
  43.7 2.5 %collective-permute-start.8 = (f32[3,256]{1,0:T(4,128)S(1)}, f32[3,256]{1,0:T(4,128)S(1)}, u32[]{:S(2)}, u32[]{:S(2)}) collective-permute-start(f32[3,256]{1,0:T(4,128)S(1)} %get-tuple-element.1218), channel_id=1, source_target_pairs={{1,0},{0,1},{3,2},{2,3},{5,4},{4,5},{7,6},{6,7},{9,8},{8,9},{11,10... | collective-permute-start | bytes 9224 | tf_op jit(solution)/shard_map/ppermute | solution.py:19
  44.7 6.4 %collective-permute-start.11 = (f32[2,3,256]{2,1,0:T(4,128)S(1)}, f32[2,3,256]{2,1,0:T(4,128)S(1)}, u32[]{:S(2)}, u32[]{:S(2)}) collective-permute-start(f32[2,3,256]{2,1,0:T(4,128)S(1)} %fusion.77), channel_id=1, source_target_pairs={{14,0},{0,2},{2,4},{4,6},{6,8},{8,10},{10,12},{12,14},{15,1},{1,3}... | collective-permute-start | bytes 18440 | tf_op jit(solution)/shard_map/ppermute | solution.py:19
  120.5 3.9 %collective-permute-start.12 = (f32[2,3,256]{2,1,0:T(4,128)S(1)}, f32[2,3,256]{2,1,0:T(4,128)S(1)}, u32[]{:S(2)}, u32[]{:S(2)}) collective-permute-start(f32[2,3,256]{2,1,0:T(4,128)S(1)} %fusion.59), channel_id=1, source_target_pairs={{2,0},{4,2},{6,4},{8,6},{10,8},{12,10},{14,12},{0,14},{3,1},{5,3},... | collective-permute-start | bytes 18440 | tf_op jit(solution)/shard_map/ppermute | solution.py:19
  122.7 2.2 collective-permute-start.13
  124.4 1.2 collective-permute-start.15
  124.4 1.3 collective-permute-start.14
  149.0 1.2 collective-permute-start.18
  149.4 1.2 collective-permute-start.17
  149.6 4.0 %collective-permute-start.16 = (f32[3,256]{1,0:T(4,128)S(1)}, f32[3,256]{1,0:T(4,128)S(1)}, u32[]{:S(2)}, u32[]{:S(2)}) collective-permute-start(f32[3,256]{1,0:T(4,128)S(1)} %get-tuple-element.1213), channel_id=1, source_target_pairs={{1,0},{0,1},{3,2},{2,3},{5,4},{4,5},{7,6},{6,7},{9,8},{8,9},{11,10... | collective-permute-start | bytes 9224 | tf_op jit(solution)/shard_map/ppermute | solution.py:19
  150.6 6.4 %collective-permute-start.19 = (f32[2,3,256]{2,1,0:T(4,128)S(1)}, f32[2,3,256]{2,1,0:T(4,128)S(1)}, u32[]{:S(2)}, u32[]{:S(2)}) collective-permute-start(f32[2,3,256]{2,1,0:T(4,128)S(1)} %fusion.75), channel_id=1, source_target_pairs={{14,0},{0,2},{2,4},{4,6},{6,8},{8,10},{10,12},{12,14},{15,1},{1,3}... | collective-permute-start | bytes 18440 | tf_op jit(solution)/shard_map/ppermute | solution.py:19
  228.3 0.7 copy-start.8
